TPU v7x, 256 devices: a whole 4x4x8 slice. The times are simulated.
256 devices in a mesh: pole: 8 (over x, y_lo), sub: 32 (over y_hi, z, core).
Axes of the slice: x: 4, y: 4 (y_hi: 2, y_lo: 2; y = y_hi * 2 + y_lo), z: 8, core: 2. Of those that a mesh axis runs over, the one named last changes fastest.
Arguments:
- start_block: float32 [131072, 128], P('sub'), may hold values from -400 to 400
- inverses: float32 [8, 256, 512, 512], P('pole', 'sub'), may hold values from -1 to 3
- iface_rows: int32 [256, 2, 128], P('sub'), may hold values from 0 to 511, as said below
- neighbors: int32 [256, 2], P('sub'), may hold values from 0 to 255, as said below
- couplings: float32 [256, 2, 128], P('sub'), may hold values from 0.25 to 1
- pole_weights: float32 [8], P('pole'), may hold values from 0.25 to 1
Outputs:
- ortho_basis: float32 [131072, 128], P(('sub', 'pole'))
Inputs may be any that keep to these rules, and one draw needn't show every extreme that they name: `iface_rows`: in each subdomain the 256 listed rows are distinct. Subdomain j lies on index j // 8 of sub. neighbors[j, 0] lies on the previous index and neighbors[j, 1] on the next one, cyclically; over the subdomains of one index, the values in column 0 are the previous index's 8 subdomains, each once, and those in column 1 the next index's, each once.
All inputs are finite; a program needn't handle non-finite values.
Results may differ from a plain program's by a relative error of at most 0.0002.
Values sent between devices are 32-bit elements; how exact they have to be, the bound alone decides.
A program may use at most 64 MiB of HBM per device.

v0:
```python
import math
import jax
import jax.numpy as jnp
from jax import lax
from jax.sharding import PartitionSpec as P

precise = lax.Precision.HIGHEST


def extended_2(cells, sides, width):
    for axis, dim in sides:
        count = lax.axis_size(axis)
        head = lax.slice_in_dim(cells, 0, width, axis=dim)
        tail = lax.slice_in_dim(cells, cells.shape[dim] - width, cells.shape[dim], axis=dim)
        cells = jnp.concatenate(
            [
                lax.ppermute(tail, axis, [(i, (i + 1) % count) for i in range(count)]),
                cells,
                lax.ppermute(head, axis, [((i + 1) % count, i) for i in range(count)]),
            ],
            axis=dim,
        )
    return cells


def apply_blocks(blocks, fields):
    return jnp.einsum(
        "sij,sjv->siv", blocks, fields, precision=precise, preferred_element_type=jnp.float32
    )


def add_coupled(fields, iface_rows, neighbor_vals, couplings):

    def one_sub(field_one, rows_one, terms_one):
        field_one = field_one.at[rows_one[0]].add(terms_one[0])
        return field_one.at[rows_one[1]].add(terms_one[1])

    return jax.vmap(one_sub)(fields, iface_rows, couplings[..., None] * neighbor_vals)


def per_device(start_block, inverses, iface_rows, neighbors, couplings, pole_weights):
    blocks = inverses[0]
    sub_count = blocks.shape[0]
    block_len = blocks.shape[1]
    vec_count = start_block.shape[1]
    iface_len = iface_rows.shape[2]
    fields = start_block.reshape(sub_count, block_len, vec_count)
    first_pass = apply_blocks(blocks, fields)
    offsets = (jnp.arange(sub_count, dtype=jnp.int32) * block_len)[:, None, None]
    flat_index = (iface_rows + offsets).transpose(1, 0, 2).reshape(-1)
    outgoing = jnp.take(first_pass.reshape(sub_count * block_len, vec_count), flat_index, axis=0)
    half_rows = sub_count * iface_len
    extended = extended_2(outgoing, (("sub", 0),), half_rows)
    from_prev = extended[:half_rows].reshape(sub_count, iface_len, vec_count)
    from_next = extended[3 * half_rows :].reshape(sub_count, iface_len, vec_count)
    columns = jnp.arange(sub_count, dtype=jnp.int32)[None, :]
    choose_prev = (neighbors[:, 0:1] % sub_count == columns).astype(jnp.float32)
    choose_next = (neighbors[:, 1:2] % sub_count == columns).astype(jnp.float32)
    low_terms = jnp.einsum(
        "jk,kiv->jiv", choose_prev, from_prev, precision=precise, preferred_element_type=jnp.float32
    )
    high_terms = jnp.einsum(
        "jk,kiv->jiv", choose_next, from_next, precision=precise, preferred_element_type=jnp.float32
    )
    corrected = add_coupled(fields, iface_rows, jnp.stack([low_terms, high_terms], 1), couplings)
    weight = pole_weights[0]
    own_rows = sub_count * block_len // lax.axis_size("pole")
    pole_term = weight * apply_blocks(blocks, corrected).reshape(sub_count * block_len, vec_count)
    summed_poles = lax.psum(pole_term, "pole")
    filtered = lax.dynamic_slice_in_dim(
        summed_poles, lax.axis_index("pole") * own_rows, own_rows, 0
    )
    local_gram = jnp.dot(
        filtered.T, filtered, precision=precise, preferred_element_type=jnp.float32
    )
    gram_matrix = lax.psum(local_gram, ("pole", "sub"))
    lower_factor = jnp.linalg.cholesky(gram_matrix)
    total_rows = sub_count * block_len * lax.axis_size("sub")
    solved = lax.linalg.triangular_solve(
        lower_factor, filtered, left_side=False, lower=True, transpose_a=True
    )
    return math.sqrt(total_rows) * solved


def solution(mesh):
    placed = (
        P("sub", None),
        P("pole", "sub", None, None),
        P("sub", None, None),
        P("sub", None),
        P("sub", None, None),
        P("pole"),
    )
    return jax.shard_map(
        per_device, mesh=mesh, in_specs=placed, out_specs=P(("sub", "pole"), None), check_vma=False
    )
```

profile of v0, /device:TPU:1, one launch (start us, length us, event | category | flops | bytes accessed | tf_op | source)
XLA Modules:
  0.0 464.7 jit_solution(7205133361967697777)
XLA Ops:
  6.5 0.0 all-reduce.3.cloned.1.call-start
  6.5 1.6 copy.37
  8.1 0.0 copy-done
  8.1 0.1 compare_and_fusion
  8.3 10.6 %fusion.2 = f32[8,512,128]{2,1,0:T(8,128)} fusion(f32[8,512,128]{2,1,0:T(8,128)S(1)} %bitcast.62, f32[1,8,512,512]{3,2,1,0:T(8,128)} %param.7), kind=kOutput, calls=%fused_computation.5 | convolution fusion | flops 3221225472 | bytes 12582912 | tf_op jit(solution)/shard_map/sij,sjv->siv/dot_general | solution.py:27
  18.8 7.0 %gather_fusion = f32[2048,128]{1,0:T(8,128)S(1)} fusion(f32[4096,128]{1,0:T(8,128)} %bitcast.64, s32[2048]{0:T(1024)S(1)} %broadcast_clamp_fusion), kind=kCustom, calls=%fused_computation | custom fusion | bytes 2105344 | tf_op jit(solution)/shard_map/jit(_take)/gather | solution.py:51
  25.9 0.0 slice-start
  25.9 0.0 copy-start.2
  25.9 0.0 copy-start.3
  25.9 0.0 copy-start.1
  25.9 0.0 copy-start.4
  25.9 0.3 broadcast_select_fusion
  26.3 1.1 fusion.27
  27.3 3.2 collective-permute-start.1
  30.5 0.0 collective-permute-start
  30.6 0.0 slice-done
  30.6 0.0 copy-done.2
  30.6 0.0 copy-done.3
  30.6 0.1 multiply_reduce_fusion
  30.7 0.0 copy-done.1
  30.7 0.1 copy.12
  31.5 0.0 copy-done.4
  31.5 0.1 and_reduce_fusion
  31.6 5.8 %collective-permute-done.1 = f32[1024,128]{1,0:T(8,128)S(1)} collective-permute-done((f32[1024,128]{1,0:T(8,128)}, f32[1024,128]{1,0:T(8,128)S(1)}, u32[]{:S(2)}, u32[]{:S(2)}) %collective-permute-start.1) | collective-permute-done | bytes 524320 | tf_op jit(solution)/shard_map/ppermute | solution.py:19
  37.4 0.7 convolution_bitcast_fusion
  38.1 0.3 collective-permute-done
  38.4 0.7 convolution_bitcast_fusion.1
  39.0 0.3 maximum_multiply_fusion
  39.4 0.1 fusion.26
  39.5 0.1 copy.16
  39.6 0.1 copy.18
  39.7 6.8 %scatter_fusion = f32[4096,128]{1,0:T(8,128)S(1)} fusion(f32[4096,128]{1,0:T(8,128)S(1)} %copy.37, s32[1024]{0:T(1024)S(1)} %get-tuple-element.18, f32[1024,128]{1,0:T(8,128)S(1)} %bitcast.67), kind=kCustom, calls=%fused_computation.1 | custom fusion | flops 131072 | bytes 1576960
  46.5 7.0 %scatter_fusion.1 = f32[4096,128]{1,0:T(8,128)S(1)} fusion(f32[4096,128]{1,0:T(8,128)S(1)} %scatter_fusion, s32[1024]{0:T(1024)S(1)} %get-tuple-element.17, f32[1024,128]{1,0:T(8,128)S(1)} %bitcast.66), kind=kCustom, calls=%fused_computation.2 | custom fusion | flops 131072 | bytes 1576960
  53.5 12.6 %multiply_bitcast_fusion = f32[8,512,128]{1,2,0:T(8,128)} fusion(f32[8,512,128]{2,1,0:T(8,128)S(1)} %bitcast.63, f32[1,8,512,512]{3,2,1,0:T(8,128)} %param.7, f32[]{:T(128)} %bitcast.61), kind=kOutput, calls=%fused_computation.7 | convolution fusion | flops 3221749760 | bytes 12582916 | tf_op jit(solution)/shard_map/sij,sjv->siv/dot_general | solution.py:27
  66.1 2.9 copy.20
  69.0 0.0 all-reduce.3.cloned.1.call-update
  69.0 0.0 all-reduce.5.cloned.1.call-start
  69.1 113.2 %all-reduce.3.cloned.1.call-done = f32[4096,128]{1,0:T(8,128)} async-done(((f32[4096,128]{1,0:T(8,128)}), f32[4096,128]{1,0:T(8,128)}) %all-reduce.3.cloned.1.call-update) | async-done | bytes 2097168 | tf_op jit(solution)/shard_map/psum | solution.py:69
  182.3 2.2 fusion.9
  184.6 0.0 all-reduce.5.cloned.1.call-update
  184.6 246.6 %all-reduce.5.cloned.1.call-done = f32[128,128]{0,1:T(8,128)} async-done(((f32[128,128]{0,1:T(8,128)}), f32[128,128]{0,1:T(8,128)}) %all-reduce.5.cloned.1.call-update) | async-done | bytes 65552 | tf_op jit(solution)/shard_map/psum | solution.py:76
  431.2 0.9 copy.22
  432.1 0.9 fusion.13
  433.0 11.7 %cholesky.16 = f32[128,128]{1,0:T(8,128)S(1)} custom-call(f32[128,128]{1,0:T(8,128)S(1)} %fusion.13), custom_call_target="Cholesky" | custom-call | tf_op jit(solution)/shard_map/jit(cholesky)/cholesky | solution.py:77
  444.8 0.6 compare_reduce_fusion
  445.4 0.7 fusion.11
  446.1 9.8 %custom-call.6 = f32[1,128,128]{1,2,0:T(8,128)S(1)} custom-call(f32[1,128,128]{2,1,0:T(8,128)S(1)} %fusion.11), custom_call_target="InvertDiagBlocksLowerTriangular" | custom-call | tf_op jit(solution)/shard_map/triangular_solve | solution.py:79
  455.9 2.0 convolution_multiply_fusion
  (11 shorter events, 0.1 us)
Async XLA Ops:
  6.5 1.6 copy-start
  6.5 175.8 %all-reduce.3.cloned.1.call-start = ((), (), s32[]{:S(2)}) async-start(), calls=%async_computation | async-start | bytes 4194304 | tf_op jit(solution)/shard_map/psum | solution.py:69
  25.9 4.7 %slice-start = ((s32[8,2,128]{2,1,0:T(2,128)}), s32[8,1,128]{2,1,0:T(1,128)S(1)}, s32[]{:S(2)}) async-start(s32[8,2,128]{2,1,0:T(2,128)} %param.8), calls=%async_computation.2 | async-start | bytes 8192 | tf_op jit(solution)/shard_map/vmap()/slice | solution.py:35
  25.9 4.7 %copy-start.2 = (s32[8,2]{0,1:T(2,128)S(1)}, s32[8,2]{0,1:T(2,128)}, u32[]{:S(2)}) copy-start(s32[8,2]{0,1:T(2,128)} %param.9) | copy-start | bytes 196
  25.9 4.7 %copy-start.3 = (s32[2]{0:T(128)S(1)}, s32[2]{0:T(128)}, u32[]{:S(2)}) copy-start(s32[2]{0:T(128)} %constant.95) | copy-start | bytes 28
  25.9 4.8 %copy-start.1 = (f32[8,2,128]{2,1,0:T(2,128)S(1)}, f32[8,2,128]{2,1,0:T(2,128)}, u32[]{:S(2)}) copy-start(f32[8,2,128]{2,1,0:T(2,128)} %param.10) | copy-start | bytes 24580
  25.9 5.6 %copy-start.4 = (s32[2]{0:T(128)S(1)}, s32[2]{0:T(128)}, u32[]{:S(2)}) copy-start(s32[2]{0:T(128)} %constant.98) | copy-start | bytes 28
  27.3 10.1 %collective-permute-start.1 = (f32[1024,128]{1,0:T(8,128)}, f32[1024,128]{1,0:T(8,128)S(1)}, u32[]{:S(2)}, u32[]{:S(2)}) collective-permute-start(f32[1024,128]{1,0:T(8,128)} %get-tuple-element.14), channel_id=1, source_target_pairs={{1,0},{2,1},{3,2},{4,3},{5,4},{6,5},{7,6},{8,7},{9,8},{10,9},{11,1... | collective-permute-start | bytes 1572872 | tf_op jit(solution)/shard_map/ppermute | solution.py:19
  30.5 7.8 %collective-permute-start = (f32[1024,128]{1,0:T(8,128)}, f32[1024,128]{1,0:T(8,128)S(1)}, u32[]{:S(2)}, u32[]{:S(2)}) collective-permute-start(f32[1024,128]{1,0:T(8,128)} %get-tuple-element.13), channel_id=1, source_target_pairs={{0,1},{1,2},{2,3},{3,4},{4,5},{5,6},{6,7},{7,8},{8,9},{9,10},{10,1... | collective-permute-start | bytes 1572872 | tf_op jit(solution)/shard_map/ppermute | solution.py:17
  69.0 362.2 %all-reduce.5.cloned.1.call-start = ((), (), s32[]{:S(2)}) async-start(), calls=%async_computation.1 | async-start | bytes 131072 | tf_op jit(solution)/shard_map/psum | solution.py:76
Sparse Core Ops, SparseCore 0:
  69.2 113.1 all-reduce.2
  187.8 243.3 all-reduce.4
where the time goes:
time: 465 us
  waiting for transfers between devices  366 us (79%)
  other arithmetic  38.4 us (8%)
  matrix products  28.8 us (6%)
  between operations  14.3 us (3%)
  local copies, waits for them, and re-layouts  14 us (3%)
    psum x1, waiting for transfers between devices, per_device(): gram_matrix = lax.psum(local_gram, ('pole', 'sub'))  247 us
    psum x1, waiting for transfers between devices, per_device(): summed_poles = lax.psum(pole_term, 'pole')  113 us
    dot_general x2, matrix products, apply_blocks(): jnp.einsum('sij,sjv->siv', blocks, fields, precision=precise, preferred_e...  23.2 us
    unnamed x5, other arithmetic  13.9 us
    another operation x3, other arithmetic, per_device(): lower_factor = jnp.linalg.cholesky(gram_matrix)  12.4 us
    another operation x2, other arithmetic, per_device(): lax.linalg.triangular_solve(lower_factor, filtered, left_side=False, lowe...  10.5 us
  transfers between devices with their start and end apart: 4, of which 4 were waited for; matrix products, arithmetic and copies ran while one was open for 0% of the time, Pallas kernels for 0%

commit v1 on v0

--- a/solution.py
+++ b/solution.py
@@ -5,6 +5,12 @@
 from jax.sharding import PartitionSpec as P
 
 precise = lax.Precision.HIGHEST
+
+
+def summed_here(x, axis):
+    shards = lax.all_gather(x, axis, axis=0, tiled=False)
+    total = shards.sum(axis=0)
+    return total
 
 
 def extended_2(cells, sides, width):
@@ -73,7 +79,7 @@
     local_gram = jnp.dot(
         filtered.T, filtered, precision=precise, preferred_element_type=jnp.float32
     )
-    gram_matrix = lax.psum(local_gram, ("pole", "sub"))
+    gram_matrix = summed_here(local_gram, ("pole", "sub"))
     lower_factor = jnp.linalg.cholesky(gram_matrix)
     total_rows = sub_count * block_len * lax.axis_size("sub")
     solved = lax.linalg.triangular_solve(

time: 465 us -> 653 us (1.40)
  waiting for transfers between devices: 366 us -> 549 us
    all_gather x0 -> x1, waiting for transfers between devices: none -> 430 us  [summed_here(): shards = lax.all_gather(x, axis, axis=0, tiled=False)]
    psum x1 -> x0, waiting for transfers between devices: 247 us -> none  [per_device(): gram_matrix = lax.psum(local_gram, ('pole', 'sub'))]
    reduce_sum x0 -> x1, other arithmetic: none -> 6.59 us  [summed_here(): total = shards.sum(axis=0)]
where the time goes in v1:
time: 653 us
  waiting for transfers between devices  549 us (84%)
  other arithmetic  44.2 us (7%)
  matrix products  28.7 us (4%)
  between operations  14.3 us (2%)
  local copies, waits for them, and re-layouts  13.2 us (2%)
    all_gather x1, waiting for transfers between devices, summed_here(): shards = lax.all_gather(x, axis, axis=0, tiled=False)  430 us
    psum x1, waiting for transfers between devices, per_device(): summed_poles = lax.psum(pole_term, 'pole')  111 us
    dot_general x2, matrix products, apply_blocks(): jnp.einsum('sij,sjv->siv', blocks, fields, precision=precise, preferred_e...  23.1 us
    unnamed x5, other arithmetic  13.9 us
  transfers between devices with their start and end apart: 4, of which 4 were waited for; matrix products, arithmetic and copies ran while one was open for 0% of the time, Pallas kernels for 0%

profile of v1, /device:TPU:1, one launch (start us, length us, event | category | flops | bytes accessed | tf_op | source)
XLA Modules:
  0.0 652.6 jit_solution(14692746117886193115)
XLA Ops:
  6.5 0.0 all-reduce.2.cloned.1.call-start
  6.5 1.6 copy.43
  8.1 0.0 copy-done
  8.1 0.1 compare_and_fusion
  8.3 10.6 %fusion.2 = f32[8,512,128]{2,1,0:T(8,128)} fusion(f32[8,512,128]{2,1,0:T(8,128)S(1)} %bitcast.63, f32[1,8,512,512]{3,2,1,0:T(8,128)} %param.7), kind=kOutput, calls=%fused_computation.5 | convolution fusion | flops 3221225472 | bytes 12582912 | tf_op jit(solution)/shard_map/sij,sjv->siv/dot_general | solution.py:33
  18.8 7.0 %gather_fusion = f32[2048,128]{1,0:T(8,128)S(1)} fusion(f32[4096,128]{1,0:T(8,128)} %bitcast.65, s32[2048]{0:T(1024)S(1)} %broadcast_clamp_fusion), kind=kCustom, calls=%fused_computation | custom fusion | bytes 2105344 | tf_op jit(solution)/shard_map/jit(_take)/gather | solution.py:57
  25.9 0.0 slice-start
  25.9 0.0 copy-start.2
  25.9 0.0 copy-start.3
  25.9 0.0 copy-start.1
  25.9 0.0 copy-start.4
  25.9 0.3 broadcast_select_fusion
  26.3 1.1 fusion.27
  27.3 3.0 collective-permute-start
  30.4 0.2 collective-permute-start.1
  30.5 0.0 slice-done
  30.6 0.0 copy-done.2
  30.6 0.0 copy-done.3
  30.6 0.1 multiply_reduce_fusion
  31.3 0.0 copy-done.1
  31.3 0.1 copy.21
  31.5 0.0 copy-done.4
  31.5 0.1 and_reduce_fusion
  31.6 5.2 collective-permute-done
  36.8 0.7 convolution_bitcast_fusion.1
  37.5 2.0 collective-permute-done.1
  39.5 0.7 convolution_bitcast_fusion
  40.1 0.3 maximum_multiply_fusion
  40.5 0.1 fusion.26
  40.6 0.1 copy.27
  40.7 0.1 copy.25
  40.8 6.8 %scatter_fusion = f32[4096,128]{1,0:T(8,128)S(1)} fusion(f32[4096,128]{1,0:T(8,128)S(1)} %copy.43, s32[1024]{0:T(1024)S(1)} %get-tuple-element.18, f32[1024,128]{1,0:T(8,128)S(1)} %bitcast.69), kind=kCustom, calls=%fused_computation.1 | custom fusion | flops 131072 | bytes 1576960
  47.6 7.0 %scatter_fusion.1 = f32[4096,128]{1,0:T(8,128)S(1)} fusion(f32[4096,128]{1,0:T(8,128)S(1)} %scatter_fusion, s32[1024]{0:T(1024)S(1)} %get-tuple-element.17, f32[1024,128]{1,0:T(8,128)S(1)} %bitcast.68), kind=kCustom, calls=%fused_computation.2 | custom fusion | flops 131072 | bytes 1576960
  54.6 12.6 %multiply_bitcast_fusion = f32[8,512,128]{1,2,0:T(8,128)} fusion(f32[8,512,128]{2,1,0:T(8,128)S(1)} %bitcast.64, f32[1,8,512,512]{3,2,1,0:T(8,128)} %param.7, f32[]{:T(128)} %bitcast.62), kind=kOutput, calls=%fused_computation.7 | convolution fusion | flops 3221749760 | bytes 12582916 | tf_op jit(solution)/shard_map/sij,sjv->siv/dot_general | solution.py:33
  67.2 2.9 copy.29
  70.1 0.0 all-reduce.2.cloned.1.call-update
  70.1 0.0 all-gather.3.cloned.1.call-start
  70.2 111.3 %all-reduce.2.cloned.1.call-done = f32[4096,128]{1,0:T(8,128)} async-done(((f32[4096,128]{1,0:T(8,128)}), f32[4096,128]{1,0:T(8,128)}) %all-reduce.2.cloned.1.call-update) | async-done | bytes 2097168 | tf_op jit(solution)/shard_map/psum | solution.py:75
  181.4 2.2 fusion.9
  183.7 0.0 all-gather.3.cloned.1.call-update
  183.7 430.5 %all-gather.3.cloned.1.call-done = f32[32768,128]{1,0:T(8,128)} async-done(((f32[128,128]{1,0:T(8,128)}), f32[32768,128]{1,0:T(8,128)}) %all-gather.3.cloned.1.call-update) | async-done | bytes 16777232 | tf_op jit(solution)/shard_map/all_gather | solution.py:11
  614.2 6.6 %reduce_sum.9 = f32[128,128]{1,0:T(8,128)S(1)} reduce(f32[256,128,128]{2,1,0:T(8,128)} %bitcast.66, f32[]{:T(128)} %constant.87.clone.1), dimensions={0}, to_apply=%region_3.4 | reduce | flops 4177920 | bytes 16842756 | tf_op jit(solution)/shard_map/reduce_sum | solution.py:12
  620.8 0.1 copy.30
  620.9 11.7 %cholesky.16 = f32[128,128]{1,0:T(8,128)S(1)} custom-call(f32[128,128]{1,0:T(8,128)S(1)} %fusion.13), custom_call_target="Cholesky" | custom-call | tf_op jit(solution)/shard_map/jit(cholesky)/cholesky | solution.py:83
  632.6 0.6 compare_reduce_fusion
  633.3 0.7 fusion.11
  633.9 9.8 %custom-call.6 = f32[1,128,128]{1,2,0:T(8,128)S(1)} custom-call(f32[1,128,128]{2,1,0:T(8,128)S(1)} %fusion.11), custom_call_target="InvertDiagBlocksLowerTriangular" | custom-call | tf_op jit(solution)/shard_map/triangular_solve | solution.py:85
  643.8 2.0 convolution_multiply_fusion
  (12 shorter events, 0.1 us)
Async XLA Ops:
  6.5 1.6 copy-start
  6.5 174.9 %all-reduce.2.cloned.1.call-start = ((), (), s32[]{:S(2)}) async-start(), calls=%async_computation | async-start | bytes 4194304 | tf_op jit(solution)/shard_map/psum | solution.py:75
  25.9 4.7 slice-start
  25.9 4.7 copy-start.2
  25.9 4.7 copy-start.3
  25.9 5.4 copy-start.1
  25.9 5.6 copy-start.4
  27.3 9.5 %collective-permute-start = (f32[1024,128]{1,0:T(8,128)}, f32[1024,128]{1,0:T(8,128)S(1)}, u32[]{:S(2)}, u32[]{:S(2)}) collective-permute-start(f32[1024,128]{1,0:T(8,128)} %get-tuple-element.13), channel_id=1, source_target_pairs={{0,1},{1,2},{2,3},{3,4},{4,5},{5,6},{6,7},{7,8},{8,9},{9,10},{10,1... | collective-permute-start | bytes 1572872 | tf_op jit(solution)/shard_map/ppermute | solution.py:23
  30.4 9.1 %collective-permute-start.1 = (f32[1024,128]{1,0:T(8,128)}, f32[1024,128]{1,0:T(8,128)S(1)}, u32[]{:S(2)}, u32[]{:S(2)}) collective-permute-start(f32[1024,128]{1,0:T(8,128)} %get-tuple-element.14), channel_id=1, source_target_pairs={{1,0},{2,1},{3,2},{4,3},{5,4},{6,5},{7,6},{8,7},{9,8},{10,9},{11,1... | collective-permute-start | bytes 1572872 | tf_op jit(solution)/shard_map/ppermute | solution.py:25
  70.1 544.1 %all-gather.3.cloned.1.call-start = ((), (), s32[]{:S(2)}) async-start(), calls=%async_computation.1 | async-start | bytes 16842752 | tf_op jit(solution)/shard_map/all_gather | solution.py:11
Sparse Core Ops, SparseCore 0:
  70.2 111.1 all-reduce.1
  183.8 430.3 all-gather.2
